TPU v7x, 512 devices: a whole 4x4x16 slice. The times are simulated.
512 devices in a mesh: lag: 64 (over z, y), par: 8 (over x, core).
Axes of the slice: x: 4, y: 4, z: 16, core: 2. Of those that a mesh axis runs over, the one named last changes fastest.
Arguments:
- prior_rows: bfloat16 [64, 512, 16384], P('lag', None, 'par'), may hold values from -0.0625 to 0.0625
- raw_rows: bfloat16 [64, 512, 16384], P('lag', None, 'par'), may hold values from -6 to 6
Outputs:
- diag_zero: float32 [64, 512, 512], P('lag', 'par')
- diag_one: float32 [64, 512, 512], P('lag', 'par')
All inputs are finite; a program needn't handle non-finite values.
Results may differ from a plain program's by a relative error of at most 0.0003.
Values may be sent and summed in bfloat16 or wider, within the bound.
No kernel may reach another device: no remote copies, remote signals or barrier semaphores. Data moves between devices by JAX's collectives and lax.ppermute only.
A program may use at most 64 MiB of HBM per device.

v0:
```python
import jax
import jax.numpy as jnp
from jax import lax
from jax.sharding import PartitionSpec as P


def passed_along(block, axis, distance):
    devices = range(lax.axis_size(axis))
    route = [(i - distance, i) for i in devices if i - distance in devices]
    return lax.ppermute(block, axis, route)


def carried_in(part, axis, combine, identity):
    place = lax.axis_index(axis)
    gathered = lax.all_gather(part, axis)
    state = jnp.zeros_like(part) + jnp.asarray(identity, part.dtype)

    def one(turn, state):
        return combine(state, lax.dynamic_index_in_dim(gathered, turn, 0, False))

    return lax.fori_loop(0, place, one, state)


def add_terms(earlier_term, later_term):
    return earlier_term + later_term


def body(prior_rows, raw_rows):
    incoming = passed_along(raw_rows, "lag", -1)
    following = jnp.concatenate([raw_rows[1:], incoming], axis=0)
    offset_zero = jnp.einsum(
        "lsp,ltp->lst", prior_rows, raw_rows, preferred_element_type=jnp.float32
    )
    offset_one = jnp.einsum(
        "lsp,ltp->lst", prior_rows, following, preferred_element_type=jnp.float32
    )
    stacked = jnp.stack([offset_zero, offset_one], axis=0)
    summed = lax.psum(stacked, "par")
    row_count = summed.shape[2] // lax.axis_size("par")
    shares = lax.dynamic_slice_in_dim(summed, lax.axis_index("par") * row_count, row_count, 2)
    running = jnp.cumsum(shares, axis=1)
    totals = running[:, -1]
    earlier = carried_in(totals, "lag", add_terms, jnp.zeros_like(totals))
    result = running + earlier[:, None]
    return (result[0], result[1])


def solution(mesh):
    in_specs = (P("lag", None, "par"), P("lag", None, "par"))
    out_specs = (P("lag", "par", None), P("lag", "par", None))
    return jax.shard_map(body, mesh=mesh, in_specs=in_specs, out_specs=out_specs, check_vma=False)
```

profile of v0, /device:TPU:504, one launch (start us, length us, event | category | flops | bytes accessed | tf_op | source)
XLA Modules:
  0.0 406.9 jit_solution(13441115809973751010)
XLA Ops:
  7.2 2.9 collective-permute-start
  10.2 2.9 fusion.6
  13.0 42.2 %collective-permute-done = bf16[1,512,2048]{2,1,0:T(8,128)(2,1)S(1)} collective-permute-done((bf16[1,512,2048]{2,1,0:T(8,128)(2,1)}, bf16[1,512,2048]{2,1,0:T(8,128)(2,1)S(1)}, u32[]{:S(2)}, u32[]{:S(2)}) %collective-permute-start) | collective-permute-done | bytes 2097184 | tf_op jit(solution)/shard_map/ppermute | solution.py:10
  55.2 1.3 fusion.11
  56.5 1.5 pad_maximum_fusion
  58.1 83.5 %all-reduce.2.cloned.1.call-done = f32[2,1,512,512]{3,2,1,0:T(8,128)} async-done(((f32[2,1,512,512]{3,2,1,0:T(8,128)}), f32[2,1,512,512]{3,2,1,0:T(8,128)}) %all-reduce.2.cloned.1.call-update) | async-done | bytes 2097168 | tf_op jit(solution)/shard_map/psum | solution.py:38
  141.5 1.7 constant_dynamic-slice_fusion
  143.2 189.3 %all-gather.3.cloned.1.call-done = f32[128,1,64,512]{3,2,1,0:T(8,128)} async-done(((f32[2,1,64,512]{3,2,1,0:T(8,128)}), f32[128,1,64,512]{3,2,1,0:T(8,128)}) %all-gather.3.cloned.1.call-update) | async-done | bytes 16777232 | tf_op jit(solution)/shard_map/all_gather | solution.py:15
  332.6 65.8 %while.10 = (s32[]{:T(128)}, f32[2,64,512]{2,1,0:T(8,128)S(1)}, s32[]{:T(128)}, f32[64,2,64,512]{3,2,1,0:T(8,128)}, s32[]{:T(128)}, /*index=5*/s32[]{:T(128)}, s32[]{:T(128)}) while((s32[]{:T(128)}, f32[2,64,512]{2,1,0:T(8,128)S(1)}, s32[]{:T(128)}, f32[64,2,64,512]{3,2,1,0:T(8,128)}, s32[]{:T(128)}, /*index=5*/s32[]{:T(128)}, s32[]{:T(128)}) %tuple.30), condition=%wide.region_2.3_spmd, body=%wide.region_1.0_spmd.sunk | while | flops 65541 | bytes 786555 | solution.py:21
  333.6 1.0 bitcast_add_fusion.3
  345.1 1.0 bitcast_add_fusion.3
  347.2 1.0 bitcast_add_fusion.3
  349.3 1.0 bitcast_add_fusion.3
  351.4 1.0 bitcast_add_fusion.3
  353.5 1.0 bitcast_add_fusion.3
  365.0 1.0 bitcast_add_fusion.3
  367.1 1.0 bitcast_add_fusion.3
  369.1 1.0 bitcast_add_fusion.3
  371.2 1.0 bitcast_add_fusion.3
  373.3 1.0 bitcast_add_fusion.3
  384.8 1.0 bitcast_add_fusion.3
  386.9 1.0 bitcast_add_fusion.3
  389.0 1.0 bitcast_add_fusion.3
  391.1 1.0 bitcast_add_fusion.3
  (57 shorter events, 50.9 us)
Async XLA Ops:
  7.2 3.0 copy-start
  7.2 134.4 %all-reduce.2.cloned.1.call-start = ((), (), s32[]{:S(2)}) async-start(), calls=%async_computation | async-start | bytes 4194304 | tf_op jit(solution)/shard_map/psum | solution.py:38
  7.2 48.0 %collective-permute-start = (bf16[1,512,2048]{2,1,0:T(8,128)(2,1)}, bf16[1,512,2048]{2,1,0:T(8,128)(2,1)S(1)}, u32[]{:S(2)}, u32[]{:S(2)}) collective-permute-start(bf16[1,512,2048]{2,1,0:T(8,128)(2,1)} %param.5), channel_id=1, source_target_pairs={{8,0},{16,8},{24,16},{32,24},{40,32},{48,40},{56,48},{64,56},{72,6... | collective-permute-start | bytes 6291464 | tf_op jit(solution)/shard_map/ppermute | solution.py:10
  58.0 274.5 %all-gather.3.cloned.1.call-start = ((), (), s32[]{:S(2)}) async-start(), calls=%async_computation.1 | async-start | bytes 17039360 | tf_op jit(solution)/shard_map/all_gather | solution.py:15
Sparse Core Ops, SparseCore 0:
  58.2 83.3 all-reduce.1
  144.5 188.0 all-gather.2
where the time goes:
time: 409 us; the launch traced here: 407 us
  waiting for transfers between devices  315 us (77%)
  other arithmetic  66.9 us (16%)
  between operations  14.1 us (3%)
  matrix products  4.16 us (1%)
    all_gather x1, waiting for transfers between devices, carried_in(): gathered = lax.all_gather(part, axis)  189 us
    psum x1, waiting for transfers between devices, body(): summed = lax.psum(stacked, 'par')  83.5 us
    add x63, other arithmetic, add_terms(): return earlier_term + later_term  64.4 us
    ppermute x1, waiting for transfers between devices, passed_along(): return lax.ppermute(block, axis, route)  42.2 us
  transfers between devices with their start and end apart: 3, of which 3 were waited for; matrix products, arithmetic and copies ran while one was open for 1% of the time, Pallas kernels for 0%

commit v1 on v0

--- a/solution.py
+++ b/solution.py
@@ -2,6 +2,23 @@
 import jax.numpy as jnp
 from jax import lax
 from jax.sharding import PartitionSpec as P
+
+
+def reach_field(mine):
+    axis_total = lax.axis_size("par")
+
+    def _map_squares(t1, piece_out):
+        if piece_out >= axis_total:
+            return t1
+        return _map_squares(
+            t1
+            + lax.ppermute(
+                t1, "par", list(map(lambda dd: (dd, dd ^ piece_out), range(axis_total)))
+            ),
+            2 * piece_out,
+        )
+
+    return _map_squares(mine, 1)
 
 
 def passed_along(block, axis, distance):
@@ -35,7 +52,7 @@
         "lsp,ltp->lst", prior_rows, following, preferred_element_type=jnp.float32
     )
     stacked = jnp.stack([offset_zero, offset_one], axis=0)
-    summed = lax.psum(stacked, "par")
+    summed = reach_field(stacked)
     row_count = summed.shape[2] // lax.axis_size("par")
     shares = lax.dynamic_slice_in_dim(summed, lax.axis_index("par") * row_count, row_count, 2)
     running = jnp.cumsum(shares, axis=1)

time: 409 us -> 434 us (1.061)
  waiting for transfers between devices: 315 us -> 329 us
  starting transfers between devices: 2.99 us -> 13.2 us
    ppermute x0 -> x3, waiting for transfers between devices: none -> 95.9 us  [_map_squares(): lax.ppermute(t1, 'par', list(map(lambda dd: (dd, dd ^ piece_out), range(a...]
    psum x1 -> x0, waiting for transfers between devices: 83.5 us -> none  [body(): summed = lax.psum(stacked, 'par')]
    ppermute x0 -> x3, starting transfers between devices: none -> 10.3 us  [_map_squares(): lax.ppermute(t1, 'par', list(map(lambda dd: (dd, dd ^ piece_out), range(a...]
    add x0 -> x3, other arithmetic: none -> 4.34 us  [_map_squares(): t1 + lax.ppermute(t1, 'par', list(map(lambda dd: (dd, dd ^ piece_out), ra...]
  transfers between devices with their start and end apart: 3 -> 5, of which waited for: 3 -> 5; matrix products, arithmetic and copies ran while one was open for 1% -> 1% of each run, Pallas kernels for 0% -> 0%
where the time goes in v1:
time: 434 us; the launch traced here: 431 us
  waiting for transfers between devices  329 us (76%)
  other arithmetic  69 us (16%)
  between operations  14.1 us (3%)
  starting transfers between devices  13.2 us (3%)
    all_gather x1, waiting for transfers between devices, carried_in(): gathered = lax.all_gather(part, axis)  191 us
    ppermute x3, waiting for transfers between devices, _map_squares(): lax.ppermute(t1, 'par', list(map(lambda dd: (dd, dd ^ piece_out), range(a...  95.9 us
    add x63, other arithmetic, add_terms(): return earlier_term + later_term  64.4 us
    ppermute x1, waiting for transfers between devices, passed_along(): return lax.ppermute(block, axis, route)  42.2 us
    ppermute x3, starting transfers between devices, _map_squares(): lax.ppermute(t1, 'par', list(map(lambda dd: (dd, dd ^ piece_out), range(a...  10.3 us
  transfers between devices with their start and end apart: 5, of which 5 were waited for; matrix products, arithmetic and copies ran while one was open for 1% of the time, Pallas kernels for 0%

profile of v1, /device:TPU:504, one launch (start us, length us, event | category | flops | bytes accessed | tf_op | source)
XLA Modules:
  0.0 431.4 jit_solution(296833538035204137)
XLA Ops:
  7.2 2.9 collective-permute-start
  10.2 2.9 fusion.6
  13.0 42.2 %collective-permute-done = bf16[1,512,2048]{2,1,0:T(8,128)(2,1)S(1)} collective-permute-done((bf16[1,512,2048]{2,1,0:T(8,128)(2,1)}, bf16[1,512,2048]{2,1,0:T(8,128)(2,1)S(1)}, u32[]{:S(2)}, u32[]{:S(2)}) %collective-permute-start) | collective-permute-done | bytes 2097184 | tf_op jit(solution)/shard_map/ppermute | solution.py:27
  55.2 1.3 fusion.11
  56.7 1.9 collective-permute-start.1
  58.6 4.1 collective-permute-done.1
  63.2 3.4 collective-permute-start.2
  66.6 46.1 %collective-permute-done.2 = f32[2,1,512,512]{3,2,1,0:T(8,128)S(1)} collective-permute-done((f32[2,1,512,512]{3,2,1,0:T(8,128)S(1)}, f32[2,1,512,512]{3,2,1,0:T(8,128)S(1)}, u32[]{:S(2)}, u32[]{:S(2)}) %collective-permute-start.2) | collective-permute-done | bytes 2097184 | tf_op jit(solution)/shard_map/ppermute | solution.py:15
  112.8 2.1 fusion.17
  114.9 4.9 %collective-permute-start.3 = (f32[2,1,512,512]{3,2,1,0:T(8,128)}, f32[2,1,512,512]{3,2,1,0:T(8,128)}, u32[]{:S(2)}, u32[]{:S(2)}) collective-permute-start(f32[2,1,512,512]{3,2,1,0:T(8,128)} %fusion.17), channel_id=1, source_target_pairs={{0,4},{1,5},{2,6},{3,7},{4,0},{5,1},{6,2},{7,3},{8,12},{9,13},{10,... | collective-permute-start | bytes 6291464 | tf_op jit(solution)/shard_map/ppermute | solution.py:15
  119.8 45.6 %collective-permute-done.3 = f32[2,1,512,512]{3,2,1,0:T(8,128)} collective-permute-done((f32[2,1,512,512]{3,2,1,0:T(8,128)}, f32[2,1,512,512]{3,2,1,0:T(8,128)}, u32[]{:S(2)}, u32[]{:S(2)}) %collective-permute-start.3) | collective-permute-done | bytes 2097184 | tf_op jit(solution)/shard_map/ppermute | solution.py:15
  165.4 1.8 dynamic-slice_add_fusion
  167.2 190.8 %all-gather.3.cloned.1.call-done = f32[128,1,64,512]{3,2,1,0:T(8,128)} async-done(((f32[2,1,64,512]{3,2,1,0:T(8,128)}), f32[128,1,64,512]{3,2,1,0:T(8,128)}) %all-gather.3.cloned.1.call-update) | async-done | bytes 16777232 | tf_op jit(solution)/shard_map/all_gather | solution.py:32
  358.0 65.8 %while.10 = (s32[]{:T(128)}, f32[2,64,512]{2,1,0:T(8,128)S(1)}, s32[]{:T(128)}, f32[64,2,64,512]{3,2,1,0:T(8,128)}, s32[]{:T(128)}, /*index=5*/s32[]{:T(128)}, s32[]{:T(128)}) while((s32[]{:T(128)}, f32[2,64,512]{2,1,0:T(8,128)S(1)}, s32[]{:T(128)}, f32[64,2,64,512]{3,2,1,0:T(8,128)}, s32[]{:T(128)}, /*index=5*/s32[]{:T(128)}, s32[]{:T(128)}) %tuple.28), condition=%wide.region_1.2_spmd, body=%wide.region_0.0_spmd.sunk | while | flops 65541 | bytes 786555 | solution.py:38
  358.0 1.1 bitcast_add_fusion.3
  362.2 1.0 bitcast_add_fusion.3
  364.3 1.0 bitcast_add_fusion.3
  366.4 1.0 bitcast_add_fusion.3
  368.5 1.0 bitcast_add_fusion.3
  370.6 1.0 bitcast_add_fusion.3
  382.1 1.0 bitcast_add_fusion.3
  384.2 1.0 bitcast_add_fusion.3
  386.3 1.0 bitcast_add_fusion.3
  388.3 1.0 bitcast_add_fusion.3
  (64 shorter events, 55.7 us)
Async XLA Ops:
  7.2 3.0 copy-start
  7.2 350.8 %all-gather.3.cloned.1.call-start = ((), (), s32[]{:S(2)}) async-start(), calls=%async_computation | async-start | bytes 17039360 | tf_op jit(solution)/shard_map/all_gather | solution.py:32
  7.2 48.0 %collective-permute-start = (bf16[1,512,2048]{2,1,0:T(8,128)(2,1)}, bf16[1,512,2048]{2,1,0:T(8,128)(2,1)S(1)}, u32[]{:S(2)}, u32[]{:S(2)}) collective-permute-start(bf16[1,512,2048]{2,1,0:T(8,128)(2,1)} %param.5), channel_id=1, source_target_pairs={{8,0},{16,8},{24,16},{32,24},{40,32},{48,40},{56,48},{64,56},{72,6... | collective-permute-start | bytes 6291464 | tf_op jit(solution)/shard_map/ppermute | solution.py:27
  56.7 6.1 %collective-permute-start.1 = (f32[2,1,512,512]{3,2,1,0:T(8,128)S(1)}, f32[2,1,512,512]{3,2,1,0:T(8,128)S(1)}, u32[]{:S(2)}, u32[]{:S(2)}) collective-permute-start(f32[2,1,512,512]{3,2,1,0:T(8,128)S(1)} %pad_maximum_fusion), channel_id=1, source_target_pairs={{0,1},{1,0},{2,3},{3,2},{4,5},{5,4},{6,7},{7,6},{8,9},{9,8},{10,11... | collective-permute-start | bytes 6291464 | tf_op jit(solution)/shard_map/ppermute | solution.py:15
  63.2 49.6 %collective-permute-start.2 = (f32[2,1,512,512]{3,2,1,0:T(8,128)S(1)}, f32[2,1,512,512]{3,2,1,0:T(8,128)S(1)}, u32[]{:S(2)}, u32[]{:S(2)}) collective-permute-start(f32[2,1,512,512]{3,2,1,0:T(8,128)S(1)} %fusion.16), channel_id=1, source_target_pairs={{0,2},{1,3},{2,0},{3,1},{4,6},{5,7},{6,4},{7,5},{8,10},{9,11},{10,... | collective-permute-start | bytes 6291464 | tf_op jit(solution)/shard_map/ppermute | solution.py:15
  114.9 50.5 %collective-permute-start.3 = (f32[2,1,512,512]{3,2,1,0:T(8,128)}, f32[2,1,512,512]{3,2,1,0:T(8,128)}, u32[]{:S(2)}, u32[]{:S(2)}) collective-permute-start(f32[2,1,512,512]{3,2,1,0:T(8,128)} %fusion.17), channel_id=1, source_target_pairs={{0,4},{1,5},{2,6},{3,7},{4,0},{5,1},{6,2},{7,3},{8,12},{9,13},{10,... | collective-permute-start | bytes 6291464 | tf_op jit(solution)/shard_map/ppermute | solution.py:15
  358.0 65.8 %copy-start.1 = (f32[2,1,64,512]{3,2,1,0:T(8,128)S(1)}, f32[2,1,64,512]{3,2,1,0:T(8,128)}, u32[]{:S(2)}) copy-start(f32[2,1,64,512]{3,2,1,0:T(8,128)} %dynamic-slice_add_fusion) | copy-start | bytes 786436
Sparse Core Ops, SparseCore 0:
  167.3 190.6 all-gather.2
